TPU v7x, 256 devices: a whole 4x4x8 slice. The times are simulated.
256 devices in a mesh: seq: 16 (over y, x), chan: 16 (over z, core).
Axes of the slice: x: 4, y: 4, z: 8, core: 2. Of those that a mesh axis runs over, the one named last changes fastest.
Arguments:
- tokens: bfloat16 [57344, 2048], P('seq', 'chan'), may hold values from -6 to 6
- w_query: bfloat16 [2048, 256], replicated, may hold values from -0.125 to 0.125
- w_key: bfloat16 [2048, 256], replicated, may hold values from -0.125 to 0.125
- w_value: bfloat16 [2048, 2048], P(None, 'chan'), may hold values from -0.125 to 0.125
- w_out: bfloat16 [2048, 2048], replicated, may hold values from -0.125 to 0.125
- gain: float32 [2048], replicated, may hold values from 0.1 to 1.9
Outputs:
- mixed: bfloat16 [57344, 2048], P('seq', 'chan')
All inputs are finite; a program needn't handle non-finite values.
Results may differ from a plain program's by a relative error of at most 0.019.
Values may be sent and summed in bfloat16 or wider, within the bound.
A program may use at most 128 MiB of HBM per device.

v0:
```python
import jax
import jax.numpy as jnp
from jax import lax
from jax.sharding import PartitionSpec as P

HEADS = 16
FEAT = 16
HEAD_DIM = 128
BLOCK = 896


def feature_parts(rows):
    linear = rows * FEAT ** (-0.25)
    square = (rows[..., :, None] * rows[..., None, :]).reshape(rows.shape[:-1] + (FEAT * FEAT,)) * (
        2.0 * FEAT
    ) ** (-0.5)
    return (linear, square)


def per_device(tokens, w_query, w_key, w_value, w_out, gain):
    highest = lax.Precision.HIGHEST
    groups = lax.axis_size("chan")
    per_group = HEADS // groups
    my_group = lax.axis_index("chan")
    my_slab = lax.axis_index("seq")
    tok_rows = tokens.shape[0]
    query_cols = per_group * FEAT
    value_cols = per_group * HEAD_DIM
    query_mine = lax.dynamic_slice_in_dim(w_query, my_group * query_cols, query_cols, 1)
    key_mine = lax.dynamic_slice_in_dim(w_key, my_group * query_cols, query_cols, 1)
    initial = (
        jnp.zeros((tok_rows, query_cols), jnp.float32),
        jnp.zeros((tok_rows, query_cols), jnp.float32),
        jnp.zeros((tok_rows, value_cols), jnp.float32),
    )
    piece = lax.all_gather(tokens, "chan", axis=1, tiled=True)
    query_sum, key_sum, value_sum = tuple(
        (
            jnp.dot(piece, weight, preferred_element_type=jnp.float32)
            for weight in (query_mine, key_mine, w_value)
        )
    )
    query_rows = query_sum.astype(jnp.bfloat16)
    key_rows = key_sum.astype(jnp.bfloat16)
    value_rows = value_sum.astype(jnp.bfloat16)
    blocks = tok_rows // BLOCK
    query_blocks = query_rows.reshape(blocks, BLOCK, per_group, FEAT)
    key_blocks = key_rows.reshape(blocks, BLOCK, per_group, FEAT)
    value_blocks = value_rows.reshape(blocks, BLOCK, per_group, HEAD_DIM)
    value_f32 = value_blocks.astype(jnp.float32)
    key_linear, key_square = feature_parts(key_blocks.astype(jnp.float32))
    own_zero = jnp.sum(value_f32, axis=1)
    own_one = jnp.einsum("bthf,bthe->bhfe", key_linear, value_f32, precision=highest)
    own_two = jnp.einsum("bthf,bthe->bhfe", key_square, value_f32, precision=highest)
    own = (own_zero, own_one, own_two)
    slab_total = tuple((jnp.sum(member, axis=0) for member in own))
    initial = tuple((jnp.zeros_like(member) for member in slab_total))
    pieces = (
        lax.all_gather(slab_total[0][None].astype(jnp.bfloat16), "seq", axis=0, tiled=True).astype(
            jnp.float32
        ),
        lax.all_gather(slab_total[1][None].astype(jnp.bfloat16), "seq", axis=0, tiled=True).astype(
            jnp.float32
        ),
        lax.all_gather(slab_total[2][None].astype(jnp.bfloat16), "seq", axis=0, tiled=True).astype(
            jnp.float32
        ),
    )
    count = pieces[0].shape[0]
    order = jnp.arange(count, dtype=jnp.int32)
    earlier_mask = order < my_slab
    prefix = tuple(
        (
            total
            + jnp.sum(
                jnp.where(earlier_mask.reshape((count,) + (1,) * (piece.ndim - 1)), piece, 0.0),
                axis=0,
            )
            for total, piece in zip(initial, pieces)
        )
    )
    earlier = tuple(
        (
            jnp.concatenate([jnp.zeros_like(member[:1]), jnp.cumsum(member, axis=0)[:-1]], axis=0)
            + base[None]
            for member, base in zip(own, prefix)
        )
    )
    query_linear, query_square = feature_parts(query_blocks.astype(jnp.float32))
    inter = earlier[0][:, None] + jnp.einsum(
        "bthf,bhfe->bthe", query_linear, earlier[1], precision=highest
    )
    inter = inter + jnp.einsum("bthf,bhfe->bthe", query_square, earlier[2], precision=highest)
    scores = jnp.einsum(
        "bthf,bshf->bhts", query_blocks, key_blocks, preferred_element_type=jnp.float32
    ) * FEAT ** (-0.5)
    kernel = 1.0 + scores + 0.5 * scores * scores
    causal = jnp.arange(BLOCK)[:, None] >= jnp.arange(BLOCK)[None, :]
    weights = jnp.where(causal, kernel, 0.0).astype(jnp.bfloat16)
    intra = jnp.einsum("bhts,bshe->bthe", weights, value_blocks, preferred_element_type=jnp.float32)
    numerator = (intra + inter).reshape(tok_rows, per_group, HEAD_DIM)
    gain_mine = lax.dynamic_slice_in_dim(gain, my_group * value_cols, value_cols, 0).reshape(
        per_group, HEAD_DIM
    )
    mean_square = jnp.mean(numerator * numerator, axis=-1, keepdims=True)
    hidden = (
        (numerator * lax.rsqrt(mean_square + 1e-05) * gain_mine)
        .astype(jnp.bfloat16)
        .reshape(tok_rows, value_cols)
    )
    out_mine = lax.dynamic_slice_in_dim(w_out, my_group * value_cols, value_cols, 0)
    partial_value = jnp.dot(hidden, out_mine, preferred_element_type=jnp.float32)
    partial_value = lax.optimization_barrier(partial_value.astype(jnp.bfloat16)).astype(jnp.float32)
    mixed = lax.psum_scatter(
        partial_value.astype(jnp.bfloat16), "chan", scatter_dimension=1, tiled=True
    )
    return mixed


def solution(mesh):
    return jax.shard_map(
        per_device,
        mesh=mesh,
        in_specs=(P("seq", "chan"), P(), P(), P(None, "chan"), P(), P()),
        out_specs=P("seq", "chan"),
        check_vma=False,
    )
```

profile of v0, /device:TPU:2, one launch (start us, length us, event | category | flops | bytes accessed | tf_op | source)
XLA Modules:
  0.0 357.5 jit_solution(1797674125439511556)
XLA Ops:
  6.5 0.7 all-gather.7.cloned.1.call-update
  7.3 0.8 dynamic_slice.14
  8.3 96.7 %all-gather.7.cloned.1.call-done = bf16[3584,2048]{1,0:T(8,128)(2,1)} async-done(((bf16[3584,128]{1,0:T(8,128)(2,1)}), bf16[3584,2048]{1,0:T(8,128)(2,1)}) %all-gather.7.cloned.1.call-update) | async-done | bytes 14680080 | tf_op jit(solution)/shard_map/all_gather | solution.py:36
  105.0 9.2 %fusion.51 = (bf16[128]{0:T(256)(128)(2,1)S(1)}, bf16[3584,128]{1,0:T(8,128)(2,1)S(1)}) fusion(bf16[3584,2048]{1,0:T(8,128)(2,1)} %all-gather.7.cloned.1.call-done, bf16[2048,128]{1,0:T(8,128)(2,1)} %param.9), kind=kOutput, calls=%fused_computation.68 | convolution fusion | flops 1879965568 | bytes 16122112 | tf_op jit(solution)/shard_map/dot_general | solution.py:39
  114.4 9.4 %convolution_convert_fusion.2 = bf16[16,3584]{1,0:T(8,128)(2,1)S(1)} fusion(bf16[3584,2048]{1,0:T(8,128)(2,1)} %all-gather.7.cloned.1.call-done, bf16[2048,256]{1,0:T(8,128)(2,1)S(1)} %copy-done, s32[]{:T(128)S(6)} %select_n.25), kind=kOutput, calls=%fused_computation.3 | convolution fusion | flops 234938368 | bytes 15319044 | tf_op jit(solution)/shard_map/dot_general | solution.py:39
  123.8 0.5 fusion.50
  124.4 20.3 %all-gather.3 = bf16[16,1,128]{2,1,0:T(2,128)(2,1)S(1)} all-gather(bf16[1,1,128]{2,1,0:T(2,128)(2,1)S(1)} %bitcast.100), channel_id=2, replica_groups=mesh['seq'=16,'chan'=16] {'seq'}, dimensions={0}, use_global_device_ids=true | all-gather | bytes 4352 | tf_op jit(solution)/shard_map/all_gather | solution.py:59
  144.8 21.4 %all-gather.1 = bf16[256,128]{1,0:T(8,128)(2,1)S(1)} all-gather(bf16[16,128]{1,0:T(8,128)(2,1)S(1)} %get-tuple-element.7), channel_id=3, replica_groups=mesh['seq'=16,'chan'=16] {'seq'}, dimensions={0}, use_global_device_ids=true | all-gather | bytes 69632 | tf_op jit(solution)/shard_map/all_gather | solution.py:62
  166.2 0.4 multiply_multiply_fusion.1
  166.6 2.5 fusion.49
  169.1 0.4 fusion.8
  169.8 9.6 %convolution_convert_fusion.3 = bf16[16,3584]{1,0:T(8,128)(2,1)S(1)} fusion(bf16[3584,2048]{1,0:T(8,128)(2,1)} %all-gather.7.cloned.1.call-done, bf16[2048,256]{1,0:T(8,128)(2,1)} %param.7, s32[]{:T(128)S(6)} %select_n.25), kind=kOutput, calls=%fused_computation.4 | convolution fusion | flops 234938368 | bytes 15319044 | tf_op jit(solution)/shard_map/dot_general | solution.py:39
  179.4 2.9 fusion.16
  182.3 2.2 multiply_multiply_fusion
  184.5 29.4 %all-gather.9.cloned.1.call-done = bf16[4096,128]{1,0:T(8,128)(2,1)} async-done(((bf16[256,128]{1,0:T(8,128)(2,1)}), bf16[4096,128]{1,0:T(8,128)(2,1)}) %all-gather.9.cloned.1.call-update) | async-done | bytes 1048592 | tf_op jit(solution)/shard_map/all_gather | solution.py:65
  213.9 1.5 fusion
  215.4 5.6 %fusion.6 = f32[4,128,896]{2,1,0:T(8,128)} fusion(f32[4,896,256]{1,2,0:T(8,128)} %bitcast.84, f32[3,1,256,128]{3,2,0,1:T(8,128)S(1)} %slice-done, f32[256,128]{1,0:T(8,128)S(1)} %fusion), kind=kOutput, calls=%fused_computation.20 | convolution fusion | flops 1409417216 | bytes 6029312 | tf_op jit(solution)/shard_map/bthf,bhfe->bthe/dot_general | solution.py:93
  221.0 8.5 %multiply_reduce_fusion = (f32[4,896]{1,0:T(4,128)S(1)}, f32[4,896,1,128]{1,3,0,2:T(8,128)}) fusion(f32[4,128,896]{2,1,0:T(8,128)} %fusion.6, f32[4,128,896]{2,1,0:T(8,128)} %fusion.16, f32[4,128]{1,0:T(4,128)S(1)} %add_bitcast_fusion, bf16[4,896,128]{2,1,0:T(8,128)(2,1)S(1)} %bitcast.88, pred[896,896]{1,0:T(8,128)(4,1)S(1)} %iota_compare_fusion, ...), kind=kOutput, calls=%fused_computation.18 | convolution fusion | flops 949613056 | bytes 7471104 | tf_op jit(solution)/shard_map/bhts,bshe->bthe/dot_general | solution.py:100
  229.5 1.8 copy.41
  231.3 0.5 fusion.3
  231.9 8.3 %convolution_convert_fusion = bf16[3584,2048]{1,0:T(8,128)(2,1)} fusion(bf16[3584,128]{1,0:T(8,128)(2,1)S(1)} %fusion.3, bf16[2048,2048]{1,0:T(8,128)(2,1)} %param.10, s32[]{:T(128)S(6)} %select_n.30), kind=kOutput, calls=%fused_computation | convolution fusion | flops 1886388224 | bytes 16121860 | tf_op jit(solution)/shard_map/dot_general | solution.py:112
  240.2 18.8 %copy.45 = bf16[3584,2048]{0,1:T(8,128)(2,1)} copy(bf16[3584,2048]{1,0:T(8,128)(2,1)} %convolution_convert_fusion) | data formatting | bytes 29360128
  259.0 89.8 %reduce-scatter.4.cloned.1.call-done = bf16[128,3584]{1,0:T(8,128)(2,1)} async-done(((bf16[2048,3584]{1,0:T(8,128)(2,1)}), bf16[128,3584]{1,0:T(8,128)(2,1)}) %reduce-scatter.4.cloned.1.call-update) | async-done | bytes 917520
  348.8 2.2 copy.46
  (29 shorter events, 0.9 us)
Async XLA Ops:
  6.5 107.9 %copy-start = (bf16[2048,256]{1,0:T(8,128)(2,1)S(1)}, bf16[2048,256]{1,0:T(8,128)(2,1)}, u32[]{:S(2)}) copy-start(bf16[2048,256]{1,0:T(8,128)(2,1)} %param.8) | copy-start | bytes 3145732
  6.5 98.5 %all-gather.7.cloned.1.call-start = ((), (), s32[]{:S(2)}) async-start(), calls=%async_computation.1 | async-start | bytes 15597568 | tf_op jit(solution)/shard_map/all_gather | solution.py:36
  7.3 206.7 %all-gather.9.cloned.1.call-start = ((), (), s32[]{:S(2)}) async-start(), calls=%async_computation.2 | async-start | bytes 1114112 | tf_op jit(solution)/shard_map/all_gather | solution.py:65
  144.8 24.3 %copy-start.3 = (f32[4,1,16,128]{3,2,0,1:T(8,128)}, f32[4,1,16,128]{3,2,0,1:T(8,128)S(1)}, u32[]{:S(2)}) copy-start(f32[4,1,16,128]{3,2,0,1:T(8,128)S(1)} %fusion.32) | copy-start | bytes 98308
  169.1 179.7 %reduce-scatter.4.cloned.1.call-start = ((), (), s32[]{:S(2)}) async-start(), calls=%async_computation.3 | async-start | bytes 15597568
  169.5 9.9 %copy-start.2 = (f32[4,1,256,128]{3,2,0,1:T(8,128)}, f32[4,1,256,128]{3,2,0,1:T(8,128)S(1)}, u32[]{:S(2)}) copy-start(f32[4,1,256,128]{3,2,0,1:T(8,128)S(1)} %fusion.8) | copy-start | bytes 1572868
  169.8 9.6 %slice-start.1 = ((f32[4,1,16,128]{3,2,0,1:T(8,128)}), f32[3,1,16,128]{3,2,0,1:T(8,128)S(1)}, s32[]{:S(2)}) async-start(f32[4,1,16,128]{3,2,0,1:T(8,128)} %copy-done.3), calls=%async_computation.5 | async-start | bytes 49152 | tf_op jit(solution)/shard_map/slice | solution.py:84
  179.4 36.0 %slice-start = ((f32[4,1,256,128]{3,2,0,1:T(8,128)}), f32[3,1,256,128]{3,2,0,1:T(8,128)S(1)}, s32[]{:S(2)}) async-start(f32[4,1,256,128]{3,2,0,1:T(8,128)} %copy-done.2), calls=%async_computation.4 | async-start | bytes 786432 | tf_op jit(solution)/shard_map/slice | solution.py:84
  259.0 92.0 %copy-start.1 = (bf16[2048,256]{1,0:T(8,128)(2,1)S(1)}, bf16[2048,256]{1,0:T(8,128)(2,1)}, u32[]{:S(2)}) copy-start(bf16[2048,256]{1,0:T(8,128)(2,1)} %param.8) | copy-start | bytes 3145732
Sparse Core Ops, SparseCore 0:
  9.1 95.8 all-gather.6
  169.2 44.6 all-gather.8
  259.1 89.6 reduce-scatter.3
where the time goes:
time: 358 us
  waiting for transfers between devices  217 us (61%)
  matrix products  56.4 us (16%)
  blocking collectives  41.7 us (12%)
  local copies, waits for them, and re-layouts  23.6 us (7%)
  between operations  13.3 us (4%)
  other arithmetic  5.75 us (2%)
    all_gather x1, waiting for transfers between devices, per_device(): piece = lax.all_gather(tokens, 'chan', axis=1, tiled=True)  96.7 us
    unnamed x4, waiting for transfers between devices  90.5 us
    all_gather x1, waiting for transfers between devices, per_device(): lax.all_gather(slab_total[2][None].astype(jnp.bfloat16), 'seq', axis=0, t...  29.4 us
    dot_general x3, matrix products, per_device(): jnp.dot(piece, weight, preferred_element_type=jnp.float32)  28.2 us
    all_gather x1, blocking collectives, per_device(): lax.all_gather(slab_total[1][None].astype(jnp.bfloat16), 'seq', axis=0, t...  21.4 us
    unnamed x10, local copies, waits for them, and re-layouts  21 us
    all_gather x1, blocking collectives, per_device(): lax.all_gather(slab_total[0][None].astype(jnp.bfloat16), 'seq', axis=0, t...  20.3 us
    dot_general x1, matrix products, per_device(): jnp.einsum('bhts,bshe->bthe', weights, value_blocks, preferred_element_ty...  8.45 us
  transfers between devices with their start and end apart: 3, of which 3 were waited for; matrix products, arithmetic and copies ran while one was open for 5% of the time, Pallas kernels for 0%

commit v1 on v0

--- a/solution.py
+++ b/solution.py
@@ -62,9 +62,15 @@
         lax.all_gather(slab_total[1][None].astype(jnp.bfloat16), "seq", axis=0, tiled=True).astype(
             jnp.float32
         ),
-        lax.all_gather(slab_total[2][None].astype(jnp.bfloat16), "seq", axis=0, tiled=True).astype(
-            jnp.float32
-        ),
+        jnp.concatenate(
+            lax.all_to_all(
+                jnp.stack([slab_total[2][None].astype(jnp.bfloat16)] * lax.axis_size("seq")),
+                "seq",
+                0,
+                0,
+            ),
+            axis=0,
+        ).astype(jnp.float32),
     )
     count = pieces[0].shape[0]
     order = jnp.arange(count, dtype=jnp.int32)

time: 358 us -> 336 us (0.939)
  waiting for transfers between devices: 217 us -> 184 us
  starting transfers between devices: 0.08 us -> 6.19 us
    all_gather x1 -> x0, waiting for transfers between devices: 29.4 us -> none  [per_device(): lax.all_gather(slab_total[2][None].astype(jnp.bfloat16), 'seq', axis=0, t...]
    all_to_all x0 -> x1, starting transfers between devices: none -> 5.97 us  [per_device(): lax.all_to_all(jnp.stack([slab_total[2][None].astype(jnp.bfloat16)] * lax...]
    unnamed x4 -> x3, waiting for transfers between devices: 90.5 us -> 87.9 us
    unnamed x10 -> x22, local copies, waits for them, and re-layouts: 21 us -> 21 us
  transfers between devices with their start and end apart: 3 -> 3, of which waited for: 3 -> 2; matrix products, arithmetic and copies ran while one was open for 5% -> 5% of each run, Pallas kernels for 0% -> 0%
where the time goes in v1:
time: 336 us; the launch traced here: 335 us
  waiting for transfers between devices  184 us (55%)
  matrix products  56.2 us (17%)
  blocking collectives  43.6 us (13%)
  local copies, waits for them, and re-layouts  25.5 us (8%)
  between operations  13.6 us (4%)
  starting transfers between devices  6.19 us (2%)
  other arithmetic  5.5 us (2%)
    all_gather x1, waiting for transfers between devices, per_device(): piece = lax.all_gather(tokens, 'chan', axis=1, tiled=True)  96.3 us
    unnamed x3, waiting for transfers between devices  87.9 us
    dot_general x3, matrix products, per_device(): jnp.dot(piece, weight, preferred_element_type=jnp.float32)  28.2 us
    all_gather x1, blocking collectives, per_device(): lax.all_gather(slab_total[1][None].astype(jnp.bfloat16), 'seq', axis=0, t...  23.3 us
    unnamed x22, local copies, waits for them, and re-layouts  21 us
    all_gather x1, blocking collectives, per_device(): lax.all_gather(slab_total[0][None].astype(jnp.bfloat16), 'seq', axis=0, t...  20.3 us
    dot_general x1, matrix products, per_device(): jnp.dot(hidden, out_mine, preferred_element_type=jnp.float32)  8.32 us
    dot_general x1, matrix products, per_device(): jnp.einsum('bhts,bshe->bthe', weights, value_blocks, preferred_element_ty...  8.24 us
  transfers between devices with their start and end apart: 3, of which 2 were waited for; matrix products, arithmetic and copies ran while one was open for 5% of the time, Pallas kernels for 0%

profile of v1, /device:TPU:2, one launch (start us, length us, event | category | flops | bytes accessed | tf_op | source)
XLA Modules:
  0.0 334.7 jit_solution(1636277537946885014)
XLA Ops:
  6.5 0.7 all-gather.5.cloned.1.call-update
  7.3 1.2 dynamic_slice.14
  8.8 96.3 %all-gather.5.cloned.1.call-done = bf16[3584,2048]{1,0:T(8,128)(2,1)} async-done(((bf16[3584,128]{1,0:T(8,128)(2,1)}), bf16[3584,2048]{1,0:T(8,128)(2,1)}) %all-gather.5.cloned.1.call-update) | async-done | bytes 14680080 | tf_op jit(solution)/shard_map/all_gather | solution.py:36
  105.0 9.2 %fusion.51 = (bf16[128]{0:T(256)(128)(2,1)S(1)}, bf16[3584,128]{1,0:T(8,128)(2,1)S(1)}) fusion(bf16[3584,2048]{1,0:T(8,128)(2,1)} %all-gather.5.cloned.1.call-done, bf16[2048,128]{1,0:T(8,128)(2,1)} %param.9), kind=kOutput, calls=%fused_computation.68 | convolution fusion | flops 1879965568 | bytes 16122112 | tf_op jit(solution)/shard_map/dot_general | solution.py:39
  114.4 9.4 %convolution_convert_fusion.2 = bf16[16,3584]{1,0:T(8,128)(2,1)S(1)} fusion(bf16[3584,2048]{1,0:T(8,128)(2,1)} %all-gather.5.cloned.1.call-done, bf16[2048,256]{1,0:T(8,128)(2,1)S(1)} %copy-done, s32[]{:T(128)S(6)} %select_n.33), kind=kOutput, calls=%fused_computation.3 | convolution fusion | flops 234938368 | bytes 15319044 | tf_op jit(solution)/shard_map/dot_general | solution.py:39
  123.8 1.1 fusion.50
  125.0 20.3 %all-gather.2 = bf16[16,1,128]{2,1,0:T(2,128)(2,1)S(1)} all-gather(bf16[1,1,128]{2,1,0:T(2,128)(2,1)S(1)} %bitcast.100), channel_id=2, replica_groups=mesh['seq'=16,'chan'=16] {'seq'}, dimensions={0}, use_global_device_ids=true | all-gather | bytes 4352 | tf_op jit(solution)/shard_map/all_gather | solution.py:59
  145.7 1.8 fusion.49
  147.8 1.2 stack.2
  149.0 6.0 %all-to-all-start = ((bf16[16,1,1,256,128]{4,3,2,1,0:T(8,128)(2,1)}), bf16[16,1,1,256,128]{4,3,2,1,0:T(8,128)(2,1)S(1)}, u32[]{:S(2)}, u32[]{:S(2)}) async-start(bf16[16,1,1,256,128]{4,3,2,1,0:T(8,128)(2,1)} %stack.2), calls=%async_computation | async-start | bytes 2097152 | tf_op jit(solution)/shard_map/all_to_all | solution.py:66
  155.2 0.6 reduce_window_sum.33
  155.9 9.6 %convolution_convert_fusion.3 = bf16[16,3584]{1,0:T(8,128)(2,1)S(1)} fusion(bf16[3584,2048]{1,0:T(8,128)(2,1)} %all-gather.5.cloned.1.call-done, bf16[2048,256]{1,0:T(8,128)(2,1)} %param.7, s32[]{:T(128)S(6)} %select_n.33), kind=kOutput, calls=%fused_computation.4 | convolution fusion | flops 234938368 | bytes 15319044 | tf_op jit(solution)/shard_map/dot_general | solution.py:39
  165.5 0.6 add_bitcast_fusion
  166.2 23.3 %all-gather.1 = bf16[256,128]{1,0:T(8,128)(2,1)S(1)} all-gather(bf16[16,128]{1,0:T(8,128)(2,1)S(1)} %copy-done.3), channel_id=3, replica_groups=mesh['seq'=16,'chan'=16] {'seq'}, dimensions={0}, use_global_device_ids=true | all-gather | bytes 69632 | tf_op jit(solution)/shard_map/all_gather | solution.py:62
  189.5 2.9 fusion.16
  192.4 2.2 multiply_multiply_fusion
  194.9 5.6 %fusion.6 = f32[4,128,896]{2,1,0:T(8,128)} fusion(f32[4,896,256]{1,2,0:T(8,128)} %bitcast.85, f32[3,1,256,128]{3,2,0,1:T(8,128)S(1)} %slice-done, f32[256,128]{1,0:T(8,128)S(1)} %fusion), kind=kOutput, calls=%fused_computation.20 | convolution fusion | flops 1409417216 | bytes 6029312 | tf_op jit(solution)/shard_map/bthf,bhfe->bthe/dot_general | solution.py:99
  200.5 8.2 %multiply_reduce_fusion = (f32[4,896]{1,0:T(4,128)S(1)}, f32[4,896,1,128]{1,3,0,2:T(8,128)}) fusion(f32[4,128,896]{2,1,0:T(8,128)} %fusion.6, f32[4,128,896]{2,1,0:T(8,128)} %fusion.16, f32[4,128]{1,0:T(4,128)S(1)} %copy-done.8, bf16[4,896,128]{2,1,0:T(8,128)(2,1)S(1)} %bitcast.89, pred[896,896]{1,0:T(8,128)(4,1)S(1)} %iota_compare_fusion, ...), kind=kOutput, calls=%fused_computation.18 | convolution fusion | flops 949613056 | bytes 7471104 | tf_op jit(solution)/shard_map/bhts,bshe->bthe/dot_general | solution.py:106
  208.8 2.0 copy.41
  210.8 0.5 fusion.3
  211.3 8.3 %convolution_convert_fusion = bf16[3584,2048]{1,0:T(8,128)(2,1)} fusion(bf16[3584,128]{1,0:T(8,128)(2,1)S(1)} %fusion.3, bf16[2048,2048]{1,0:T(8,128)(2,1)} %param.10, s32[]{:T(128)S(6)} %select_n.38), kind=kOutput, calls=%fused_computation | convolution fusion | flops 1886388224 | bytes 16121860 | tf_op jit(solution)/shard_map/dot_general | solution.py:118
  219.7 18.8 %copy.45 = bf16[3584,2048]{0,1:T(8,128)(2,1)} copy(bf16[3584,2048]{1,0:T(8,128)(2,1)} %convolution_convert_fusion) | data formatting | bytes 29360128
  238.5 87.2 %reduce-scatter.4.cloned.1.call-done = bf16[128,3584]{1,0:T(8,128)(2,1)} async-done(((bf16[2048,3584]{1,0:T(8,128)(2,1)}), bf16[128,3584]{1,0:T(8,128)(2,1)}) %reduce-scatter.4.cloned.1.call-update) | async-done | bytes 917520
  325.6 2.2 copy.46
  (40 shorter events, 1.9 us)
Async XLA Ops:
  6.5 107.9 %copy-start = (bf16[2048,256]{1,0:T(8,128)(2,1)S(1)}, bf16[2048,256]{1,0:T(8,128)(2,1)}, u32[]{:S(2)}) copy-start(bf16[2048,256]{1,0:T(8,128)(2,1)} %param.8) | copy-start | bytes 3145732
  6.5 98.5 %all-gather.5.cloned.1.call-start = ((), (), s32[]{:S(2)}) async-start(), calls=%async_computation.2 | async-start | bytes 15597568 | tf_op jit(solution)/shard_map/all_gather | solution.py:36
  8.5 147.3 %copy-start.5 = (pred[16]{0:T(512)(128)(4,1)}, pred[16]{0:T(512)(128)(4,1)S(1)}, u32[]{:S(2)}) copy-start(pred[16]{0:T(512)(128)(4,1)S(1)} %iota_compare_fusion.1) | copy-start | bytes 52
  147.8 18.4 %copy-start.2 = (f32[4,1,256,128]{3,2,0,1:T(8,128)}, f32[4,1,256,128]{3,2,0,1:T(8,128)S(1)}, u32[]{:S(2)}) copy-start(f32[4,1,256,128]{3,2,0,1:T(8,128)S(1)} %fusion.8) | copy-start | bytes 1572868
  149.0 45.6 %all-to-all-start = ((bf16[16,1,1,256,128]{4,3,2,1,0:T(8,128)(2,1)}), bf16[16,1,1,256,128]{4,3,2,1,0:T(8,128)(2,1)S(1)}, u32[]{:S(2)}, u32[]{:S(2)}) async-start(bf16[16,1,1,256,128]{4,3,2,1,0:T(8,128)(2,1)} %stack.2), calls=%async_computation | async-start | bytes 2097152 | tf_op jit(solution)/shard_map/all_to_all | solution.py:66
  155.0 170.7 %reduce-scatter.4.cloned.1.call-start = ((), (), s32[]{:S(2)}) async-start(), calls=%async_computation.3 | async-start | bytes 15597568
  155.9 9.6 %copy-start.4 = (f32[4,1,128]{2,0,1:T(4,128)S(1)}, f32[4,1,128]{2,0,1:T(4,128)}, u32[]{:S(2)}) copy-start(f32[4,1,128]{2,0,1:T(4,128)} %reduce_window_sum.33) | copy-start | bytes 6148
  155.9 10.2 %copy-start.3 = (bf16[16,128]{1,0:T(8,128)(2,1)S(1)}, bf16[16,128]{1,0:T(8,128)(2,1)}, u32[]{:S(2)}) copy-start(bf16[16,128]{1,0:T(8,128)(2,1)} %get-tuple-element.7) | copy-start | bytes 12292
  155.9 33.5 %copy-start.6 = (pred[16]{0:T(512)(128)(4,1)S(1)}, pred[16]{0:T(512)(128)(4,1)}, u32[]{:S(2)}) copy-start(pred[16]{0:T(512)(128)(4,1)} %copy-done.5) | copy-start | bytes 52
  166.2 28.5 %copy-start.7 = (pred[16]{0:T(512)(128)(4,1)S(1)}, pred[16]{0:T(512)(128)(4,1)}, u32[]{:S(2)}) copy-start(pred[16]{0:T(512)(128)(4,1)} %copy-done.5) | copy-start | bytes 52
  189.5 5.4 %slice-start = ((f32[4,1,256,128]{3,2,0,1:T(8,128)}), f32[3,1,256,128]{3,2,0,1:T(8,128)S(1)}, s32[]{:S(2)}) async-start(f32[4,1,256,128]{3,2,0,1:T(8,128)} %copy-done.2), calls=%async_computation.4 | async-start | bytes 786432 | tf_op jit(solution)/shard_map/slice | solution.py:90
  194.6 5.9 %copy-start.8 = (f32[4,128]{1,0:T(4,128)S(1)}, f32[4,128]{1,0:T(4,128)}, u32[]{:S(2)}) copy-start(f32[4,128]{1,0:T(4,128)} %add_bitcast_fusion) | copy-start | bytes 6148
  208.7 2.1 copy-start.9
  238.5 89.4 %copy-start.1 = (bf16[2048,256]{1,0:T(8,128)(2,1)S(1)}, bf16[2048,256]{1,0:T(8,128)(2,1)}, u32[]{:S(2)}) copy-start(bf16[2048,256]{1,0:T(8,128)(2,1)} %param.8) | copy-start | bytes 3145732
Sparse Core Ops, SparseCore 0:
  9.1 95.8 all-gather.4
  238.6 86.9 reduce-scatter.3
